TPU v7x, 128 devices: a whole 4x4x4 slice. The times are simulated.
128 devices in a mesh: lat: 16 (over x, y), var: 8 (over z, core).
Axes of the slice: x: 4, y: 4, z: 4, core: 2. Of those that a mesh axis runs over, the one named last changes fastest.
Arguments:
- patches: bfloat16 [96, 192, 1024], P('lat', 'var'), may hold values from -6 to 6
- norm_gain: float32 [1024], replicated, may hold values from 0.25 to 1.75
- input_proj: bfloat16 [1024, 3072], replicated, may hold values from -7 to 7
- output_proj: bfloat16 [1024, 1024], replicated, may hold values from -0.1875 to 0.1875
- level_scale: float32 [40, 1024], P('var'), may hold values from 0.1 to 1.9
- level_shift: float32 [40, 1024], P('var'), may hold values from -3 to 3
- head_weight: bfloat16 [40, 1024, 320], P('var', 'lat'), may hold values from -0.1875 to 0.1875
- targets: bfloat16 [40, 96, 192, 320], P('var', 'lat'), may hold values from -6 to 6
- level_counts: int32 [4], replicated, may hold values from 13 to 37
- tile_dataset: int32 [16, 8], P('lat'), may hold values from 0 to 3
- slot_level: int32 [40], P('var'), may hold values from 0 to 39, as said below
Outputs:
- latent: bfloat16 [96, 192, 1024], P('lat', 'var')
- grad_latent: bfloat16 [96, 192, 1024], P('lat', 'var')
- grad_head: float32 [40, 1024, 320], P('var', 'lat')
Inputs may be any that keep to these rules, and one draw needn't show every extreme that they name: `slot_level`: for each j, slots j * 5 to (j + 1) * 5 - 1 hold the levels j * 5 to (j + 1) * 5 - 1 in some order.
All inputs are finite; a program needn't handle non-finite values.
Results may differ from a plain program's by a relative error of at most 0.012.
Values may be sent and summed in bfloat16 or wider, within the bound.
A program may use at most 128 MiB of HBM per device.

v0:
```python
import math
import jax
import jax.numpy as jnp
from jax import lax
from jax.sharding import PartitionSpec as P

HEADS = 16
WH = 6
WW = 12
EPS = 1e-05


def padded(array, sides, width, wrap):
    for axis, dim in sides:
        size, length = (lax.axis_size(axis), array.shape[dim])
        up = [(i, (i + 1) % size) for i in range(size if wrap else size - 1)]
        down = [(j, i) for i, j in up]
        last = lax.slice_in_dim(array, length - width, length, axis=dim)
        initial = lax.slice_in_dim(array, 0, width, axis=dim)
        before = lax.ppermute(last, axis, up)
        after = lax.ppermute(initial, axis, down)
        array = jnp.concatenate([before, array, after], axis=dim)
    return array


def layer_norm(values, gain):
    wide = values.astype(jnp.float32)
    average = jnp.mean(wide, axis=-1, keepdims=True)
    centred = wide - average
    variance = jnp.mean(centred * centred, axis=-1, keepdims=True)
    return (centred * lax.rsqrt(variance + EPS) * gain).astype(jnp.bfloat16)


def window_attention(query_ext, keyval, row_valid, heads):
    ext_rows, ext_cols, width = query_ext.shape
    head_size = width // heads
    win_rows = ext_rows // WH
    win_cols = ext_cols // WW

    def split(values, parts):
        shaped = values.reshape(win_rows, WH, win_cols, WW, parts, heads, head_size)
        return shaped.transpose(0, 2, 1, 3, 4, 5, 6).reshape(
            win_rows * win_cols, WH * WW, parts, heads, head_size
        )

    query_win = split(query_ext, 1)[:, :, 0]
    pairs = split(keyval, 2)
    key_win = pairs[:, :, 0]
    value_win = pairs[:, :, 1]
    key_mask = jnp.broadcast_to(
        row_valid.reshape(win_rows, 1, WH, 1), (win_rows, win_cols, WH, WW)
    ).reshape(win_rows * win_cols, WH * WW)
    scores = jnp.einsum(
        "wqhd,wkhd->whqk", query_win, key_win, preferred_element_type=jnp.float32
    ) / math.sqrt(head_size)
    scores = jnp.where(key_mask[:, None, None, :], scores, -jnp.inf)
    peak = jnp.max(scores, axis=-1, keepdims=True)
    weights = jnp.exp(scores - peak)
    probs = (weights / jnp.sum(weights, axis=-1, keepdims=True)).astype(jnp.bfloat16)
    mixed = jnp.einsum("whqk,wkhd->wqhd", probs, value_win, preferred_element_type=jnp.float32)
    return (
        mixed.reshape(win_rows, win_cols, WH, WW, width)
        .transpose(0, 2, 1, 3, 4)
        .reshape(ext_rows, ext_cols, width)
    )


def slot_terms(piece, target_rows, live_cols, level_scale, level_shift, heads_full):
    piece_wide = piece.astype(jnp.float32)
    rows = (
        piece_wide[None] * level_scale[:, None, None, :] + level_shift[:, None, None, :]
    ).astype(jnp.bfloat16)
    predicted = jnp.einsum("krnd,kdo->krno", rows, heads_full, preferred_element_type=jnp.float32)
    errors = ((predicted - target_rows.astype(jnp.float32)) * live_cols[:, None, :, None]).astype(
        jnp.bfloat16
    )
    back_grad = jnp.einsum("krno,kdo->krnd", errors, heads_full, preferred_element_type=jnp.float32)
    piece_grad = jnp.sum(back_grad * level_scale[:, None, None, :], axis=0)
    head_add = jnp.einsum("krnd,krno->dko", rows, errors, preferred_element_type=jnp.float32)
    return (piece_grad, head_add)


def local(
    patches,
    norm_gain,
    input_proj,
    output_proj,
    level_scale,
    level_shift,
    head_weight,
    targets,
    level_counts,
    tile_dataset,
    slot_level,
):
    band_rows, band_cols, width = patches.shape
    half_rows = WH // 2
    half_cols = WW // 2
    lat_count = lax.axis_size("lat")
    var_count = lax.axis_size("var")
    lat_place = lax.axis_index("lat")
    ext_rows = band_rows + WH
    ext_cols = band_cols + WW
    extended = padded(patches, (("lat", 0),), half_rows, False)
    extended = padded(extended, (("var", 1),), half_cols, True)
    normed_ext = layer_norm(extended, norm_gain)
    keyval = jnp.dot(
        normed_ext.reshape(-1, width), input_proj[:, width:], preferred_element_type=jnp.float32
    )
    keyval = keyval.astype(jnp.bfloat16).reshape(ext_rows, ext_cols, 2 * width)
    normed = normed_ext[half_rows : half_rows + band_rows, half_cols : half_cols + band_cols]
    queries = jnp.dot(
        normed.reshape(-1, width), input_proj[:, :width], preferred_element_type=jnp.float32
    )
    queries = queries.astype(jnp.bfloat16).reshape(band_rows, band_cols, width)
    query_ext = jnp.pad(queries, ((half_rows, WH - half_rows), (half_cols, WW - half_cols), (0, 0)))
    global_row = lat_place * band_rows - half_rows + jnp.arange(ext_rows, dtype=jnp.int32)
    row_valid = (global_row >= 0) & (global_row < lat_count * band_rows)
    mixed = window_attention(query_ext, keyval, row_valid, HEADS)
    attn = mixed[half_rows : half_rows + band_rows, half_cols : half_cols + band_cols].astype(
        jnp.bfloat16
    )
    update = jnp.dot(
        attn.reshape(-1, width), output_proj, preferred_element_type=jnp.float32
    ).reshape(band_rows, band_cols, width)
    latent = (patches.astype(jnp.float32) + update).astype(jnp.bfloat16)
    dataset_row = tile_dataset[0]
    dataset_ids = jnp.arange(level_counts.shape[0], dtype=jnp.int32)
    tile_levels = jnp.sum(
        jnp.where(dataset_row[:, None] == dataset_ids[None, :], level_counts[None, :], 0), axis=1
    )
    live_tiles = (slot_level[None, :] < tile_levels[:, None]).astype(jnp.float32)
    heads_full = lax.all_gather(head_weight, "lat", axis=1, tiled=True)
    tile_ids = jnp.arange(var_count, dtype=jnp.int32)
    piece = lax.all_gather(latent, "var", axis=1, tiled=True)
    piece_cols = piece.shape[1]
    column_tile = jnp.arange(piece_cols, dtype=jnp.int32) // band_cols
    onehot = (column_tile[:, None] == tile_ids[None, :]).astype(jnp.float32)
    column_live = jnp.dot(onehot, live_tiles)
    piece_grad, head_add = slot_terms(
        piece, targets, column_live.T, level_scale, level_shift, heads_full
    )
    latent_terms = piece_grad
    latent_terms, head_terms = (latent_terms, head_add)
    grad_latent = lax.psum_scatter(
        latent_terms.astype(jnp.bfloat16), "var", scatter_dimension=1, tiled=True
    )
    head_terms = head_terms * (1.0 / math.sqrt(lat_count * band_rows * var_count * band_cols))
    share_rows = width // lat_count
    summed = lax.psum(head_terms.astype(jnp.bfloat16), "lat").astype(jnp.float32)
    mine = lax.dynamic_slice_in_dim(summed, lat_place * share_rows, share_rows, 0)
    grad_head = jnp.transpose(mine, (1, 0, 2))
    return (latent, grad_latent, grad_head)


def solution(mesh):
    in_specs = (
        P("lat", "var", None),
        P(),
        P(),
        P(),
        P("var", None),
        P("var", None),
        P("var", "lat", None),
        P("var", "lat", None, None),
        P(),
        P("lat", None),
        P("var"),
    )
    out_specs = (P("lat", "var", None), P("lat", "var", None), P("var", "lat", None))
    return jax.shard_map(local, mesh=mesh, in_specs=in_specs, out_specs=out_specs, check_vma=False)
```

profile of v0, /device:TPU:0, one launch (start us, length us, event | category | flops | bytes accessed | tf_op | source)
XLA Modules:
  0.0 327.8 jit_solution(17000856274102400193)
XLA Ops:
  8.4 3.6 %collective-permute-start = (bf16[3,24,1024]{2,1,0:T(8,128)(2,1)S(1)}, bf16[3,24,1024]{2,1,0:T(8,128)(2,1)S(1)}, u32[]{:S(2)}, u32[]{:S(2)}) collective-permute-start(bf16[3,24,1024]{2,1,0:T(8,128)(2,1)S(1)} %get-tuple-element.25), channel_id=1, source_target_pairs={{0,8},{8,16},{16,24},{24,32},{32,40},{40,48},{48,56},{56,64},{64,7... | collective-permute-start | bytes 442376 | tf_op jit(solution)/shard_map/ppermute | solution.py:20
  16.0 3.1 collective-permute-done.1
  19.3 2.9 collective-permute-start.3
  22.4 3.2 collective-permute-done.2
  29.8 2.6 reshape.102
  38.0 3.2 copy.47
  41.2 5.5 %fusion.15 = bf16[432,2048]{1,0:T(8,128)(2,1)} fusion(bf16[1024,3072]{1,0:T(8,128)(2,1)} %param.13, f32[432,1024]{1,0:T(8,128)S(1)} %copy-done.3, f32[1024]{0:T(1024)S(1)} %copy-done.5, f32[432]{0:T(512)S(1)} %rsqrt.13, f32[432]{0:T(512)S(1)} %div.33), kind=kOutput, calls=%fused_computation.22 | convolution fusion | flops 1814593536 | bytes 7740800 | tf_op jit(solution)/shard_map/dot_general | solution.py:107
  46.8 6.4 %reshape_reshape.3 = bf16[2,6,3,12,2,16,64]{6,5,4,3,2,1,0:T(8,128)(2,1)} reshape(bf16[432,2048]{1,0:T(8,128)(2,1)} %fusion.15) | data formatting | bytes 3538944 | tf_op jit(solution)/shard_map/reshape;reshape | solution.py:41
  53.1 2.6 copy.45
  55.8 2.7 fusion.59
  58.4 4.0 %copy.59 = bf16[6,72,1,16,64]{1,4,3,0,2:T(8,128)(2,1)} copy(bf16[6,72,1,16,64]{4,3,2,1,0:T(8,128)(2,1)} %get-tuple-element.18) | data formatting | bytes 1769472
  62.5 4.0 %copy.60 = bf16[6,72,1,16,64]{1,4,3,0,2:T(8,128)(2,1)} copy(bf16[6,72,1,16,64]{4,3,2,1,0:T(8,128)(2,1)} %get-tuple-element.19) | data formatting | bytes 1769472
  66.5 3.1 fusion.25
  73.3 4.0 %copy.51 = bf16[6,72,16,64]{3,2,1,0:T(8,128)(2,1)} copy(bf16[6,72,16,64]{1,3,2,0:T(8,128)(2,1)} %fusion.34) | data formatting | bytes 1769472 | tf_op jit(solution)/shard_map/whqk,wkhd->wqhd/transpose | solution.py:60
  77.3 3.9 %reshape.100 = bf16[2,3,6,12,1024]{4,3,2,1,0:T(8,128)(2,1)} reshape(bf16[6,72,16,64]{3,2,1,0:T(8,128)(2,1)} %copy.51) | data formatting | bytes 1769472 | tf_op jit(solution)/shard_map/reshape | solution.py:62
  83.7 2.3 fusion.43
  87.1 28.4 %all-gather.3.cloned.1.call-done = bf16[6,192,1024]{2,1,0:T(8,128)(2,1)} async-done(((bf16[6,24,1024]{2,1,0:T(8,128)(2,1)}), bf16[6,192,1024]{2,1,0:T(8,128)(2,1)}) %all-gather.3.cloned.1.call-update) | async-done | bytes 2359312 | tf_op jit(solution)/shard_map/all_gather | solution.py:135
  115.6 4.4 %convert_element_type.69 = f32[6,192,1024]{2,1,0:T(8,128)} convert(bf16[6,192,1024]{2,1,0:T(8,128)(2,1)} %all-gather.3.cloned.1.call-done) | non-fusion elementwise | flops 1179648 | bytes 7077888 | tf_op jit(solution)/shard_map/convert_element_type | solution.py:69
  119.9 48.6 %all-gather.5.cloned.1.call-done = bf16[5,1024,320]{2,1,0:T(8,128)(2,1)} async-done(((bf16[5,64,320]{2,1,0:T(8,128)(2,1)}), bf16[5,1024,320]{2,1,0:T(8,128)(2,1)}) %all-gather.5.cloned.1.call-update) | async-done | bytes 3276816 | tf_op jit(solution)/shard_map/all_gather | solution.py:133
  168.5 10.1 %multiply_convert_fusion = bf16[5,6,192,320]{3,2,1,0:T(8,128)(2,1)S(1)} fusion(bf16[5,6,192,320]{3,2,1,0:T(8,128)(2,1)} %param.18, f32[5,192]{1,0:T(8,128)S(1)} %fusion.52, bf16[5,1024,320]{2,1,0:T(8,128)(2,1)} %all-gather.5.cloned.1.call-done, f32[5,1024]{1,0:T(8,128)S(1)} %copy-done.6, f32[5,1024]{1,0:T(8,128)S(1)} %copy-done.7, ...), kind=kOutput, calls=%fused_computation.11 | convolution fusion | flops 3799941120 | bytes 15412992 | tf_op jit(solution)/shard_map/krnd,kdo->krno/dot_general | solution.py:73
  180.8 6.6 %fusion.14 = bf16[1024,5,320]{0,2,1:T(8,128)(2,1)} fusion(bf16[5,6,192,320]{3,2,1,0:T(8,128)(2,1)S(1)} %multiply_convert_fusion, f32[5,1024]{1,0:T(8,128)S(1)} %copy-done.6, f32[5,1024]{1,0:T(8,128)S(1)} %copy-done.7, f32[6,192,1024]{2,1,0:T(8,128)S(1)} %copy-done.2), kind=kOutput, calls=%fused_computation.21 | convolution fusion | flops 3795845120 | bytes 11722752 | tf_op jit(solution)/shard_map/krnd,krno->dko/dot_general | solution.py:79
  187.5 9.9 %multiply_reduce_fusion = bf16[6,192,1024]{2,1,0:T(8,128)(2,1)S(1)} fusion(f32[5,1024]{1,0:T(8,128)S(1)} %copy-done.7, bf16[5,6,192,320]{3,2,1,0:T(8,128)(2,1)} %copy-done.11, bf16[5,1024,320]{2,1,0:T(8,128)(2,1)} %all-gather.5.cloned.1.call-done), kind=kOutput, calls=%fused_computation.1 | convolution fusion | flops 3785490432 | bytes 9342976 | tf_op jit(solution)/shard_map/krno,kdo->krnd/dot_general | solution.py:77
  199.1 84.3 %all-reduce.3.cloned.1.call-done = bf16[1024,5,320]{0,2,1:T(8,128)(2,1)} async-done(((bf16[1024,5,320]{0,2,1:T(8,128)(2,1)}), bf16[1024,5,320]{0,2,1:T(8,128)(2,1)}) %all-reduce.3.cloned.1.call-update) | async-done | bytes 3276816 | tf_op jit(solution)/shard_map/psum | solution.py:150
  285.6 33.4 %reduce-scatter.4.cloned.1.call-done = bf16[24,6144]{1,0:T(8,128)(2,1)} async-done(((bf16[192,6144]{1,0:T(8,128)(2,1)}), bf16[24,6144]{1,0:T(8,128)(2,1)}) %reduce-scatter.4.cloned.1.call-update) | async-done | bytes 294928
  (68 shorter events, 30.9 us)
Async XLA Ops:
  7.2 76.5 %copy-start = (bf16[1024,1024]{1,0:T(8,128)(2,1)S(1)}, bf16[1024,1024]{1,0:T(8,128)(2,1)}, u32[]{:S(2)}) copy-start(bf16[1024,1024]{1,0:T(8,128)(2,1)} %param.14) | copy-start | bytes 6291460
  7.2 108.4 %all-gather.3.cloned.1.call-start = ((), (), s32[]{:S(2)}) async-start(), calls=%async_computation.1 | async-start | bytes 2654208 | tf_op jit(solution)/shard_map/all_gather | solution.py:135
  8.4 6.7 %collective-permute-start = (bf16[3,24,1024]{2,1,0:T(8,128)(2,1)S(1)}, bf16[3,24,1024]{2,1,0:T(8,128)(2,1)S(1)}, u32[]{:S(2)}, u32[]{:S(2)}) collective-permute-start(bf16[3,24,1024]{2,1,0:T(8,128)(2,1)S(1)} %get-tuple-element.25), channel_id=1, source_target_pairs={{0,8},{8,16},{16,24},{24,32},{32,40},{40,48},{48,56},{56,64},{64,7... | collective-permute-start | bytes 442376 | tf_op jit(solution)/shard_map/ppermute | solution.py:20
  12.0 7.2 %collective-permute-start.1 = (bf16[3,24,1024]{2,1,0:T(8,128)(2,1)S(1)}, bf16[3,24,1024]{2,1,0:T(8,128)(2,1)S(1)}, u32[]{:S(2)}, u32[]{:S(2)}) collective-permute-start(bf16[3,24,1024]{2,1,0:T(8,128)(2,1)S(1)} %get-tuple-element.24), channel_id=1, source_target_pairs={{8,0},{16,8},{24,16},{32,24},{40,32},{48,40},{56,48},{64,56},{72,6... | collective-permute-start | bytes 442376 | tf_op jit(solution)/shard_map/ppermute | solution.py:21
  19.2 6.3 %collective-permute-start.2 = (bf16[12,6,1024]{2,1,0:T(8,128)(2,1)S(1)}, bf16[12,6,1024]{2,1,0:T(8,128)(2,1)S(1)}, u32[]{:S(2)}, u32[]{:S(2)}) collective-permute-start(bf16[12,6,1024]{2,1,0:T(8,128)(2,1)S(1)} %get-tuple-element.22), channel_id=1, source_target_pairs={{0,1},{1,2},{2,3},{3,4},{4,5},{5,6},{6,7},{7,0},{8,9},{9,10},{10,1... | collective-permute-start | bytes 442376 | tf_op jit(solution)/shard_map/ppermute | solution.py:20
  19.3 6.3 %collective-permute-start.3 = (bf16[12,6,1024]{2,1,0:T(8,128)(2,1)S(1)}, bf16[12,6,1024]{2,1,0:T(8,128)(2,1)S(1)}, u32[]{:S(2)}, u32[]{:S(2)}) collective-permute-start(bf16[12,6,1024]{2,1,0:T(8,128)(2,1)S(1)} %get-tuple-element.23), channel_id=1, source_target_pairs={{1,0},{2,1},{3,2},{4,3},{5,4},{6,5},{7,6},{0,7},{9,8},{10,9},{11,1... | collective-permute-start | bytes 442376 | tf_op jit(solution)/shard_map/ppermute | solution.py:21
  27.9 4.4 %copy-start.5 = (f32[1024]{0:T(1024)S(1)}, f32[1024]{0:T(1024)}, u32[]{:S(2)}) copy-start(f32[1024]{0:T(1024)} %param.12) | copy-start | bytes 12292
  38.0 3.2 copy-start.3
  69.6 1.8 copy-start.4
  82.6 4.2 %copy-start.8 = (s32[4]{0:T(128)S(1)}, s32[4]{0:T(128)}, u32[]{:S(2)}) copy-start(s32[4]{0:T(128)} %param.19) | copy-start | bytes 52
  82.6 4.2 %copy-start.9 = (s32[1,8]{1,0:T(1,128)S(1)}, s32[1,8]{1,0:T(1,128)}, u32[]{:S(2)}) copy-start(s32[1,8]{1,0:T(1,128)} %param.20) | copy-start | bytes 100
  82.6 4.3 %copy-start.10 = (s32[5]{0:T(128)S(1)}, s32[5]{0:T(128)}, u32[]{:S(2)}) copy-start(s32[5]{0:T(128)} %param.21) | copy-start | bytes 64
  86.0 82.5 %all-gather.5.cloned.1.call-start = ((), (), s32[]{:S(2)}) async-start(), calls=%async_computation.2 | async-start | bytes 4177920 | tf_op jit(solution)/shard_map/all_gather | solution.py:133
  86.7 196.6 %all-reduce.3.cloned.1.call-start = ((), (), s32[]{:S(2)}) async-start(), calls=%async_computation.3 | async-start | bytes 6553600 | tf_op jit(solution)/shard_map/psum | solution.py:150
  87.1 81.4 %copy-start.6 = (f32[5,1024]{1,0:T(8,128)S(1)}, f32[5,1024]{1,0:T(8,128)}, u32[]{:S(2)}) copy-start(f32[5,1024]{1,0:T(8,128)} %param.16) | copy-start | bytes 61444
  87.1 81.4 %copy-start.7 = (f32[5,1024]{1,0:T(8,128)S(1)}, f32[5,1024]{1,0:T(8,128)}, u32[]{:S(2)}) copy-start(f32[5,1024]{1,0:T(8,128)} %param.15) | copy-start | bytes 61444
  168.5 12.3 %copy-start.2 = (f32[6,192,1024]{2,1,0:T(8,128)S(1)}, f32[6,192,1024]{2,1,0:T(8,128)}, u32[]{:S(2)}) copy-start(f32[6,192,1024]{2,1,0:T(8,128)} %convert_element_type.69) | copy-start | bytes 14155780
  178.6 2.2 copy-start.11
  187.4 131.6 %reduce-scatter.4.cloned.1.call-start = ((), (), s32[]{:S(2)}) async-start(), calls=%async_computation.4 | async-start | bytes 2654208
  197.4 123.9 %copy-start.1 = (bf16[1024,1024]{1,0:T(8,128)(2,1)S(1)}, bf16[1024,1024]{1,0:T(8,128)(2,1)}, u32[]{:S(2)}) copy-start(bf16[1024,1024]{1,0:T(8,128)(2,1)} %param.14) | copy-start | bytes 6291460
Sparse Core Ops, SparseCore 0:
  86.1 29.4 all-gather.2
  117.7 50.7 all-gather.4
  187.6 95.7 all-reduce.2
  285.8 33.2 reduce-scatter.3
where the time goes:
time: 329 us; the launch traced here: 328 us
  waiting for transfers between devices  204 us (62%)
  local copies, waits for them, and re-layouts  48 us (15%)
  matrix products  41.6 us (13%)
  between operations  14 us (4%)
  other arithmetic  12.7 us (4%)
  starting transfers between devices  7.98 us (2%)
    psum x1, waiting for transfers between devices, local(): lax.psum(head_terms.astype(jnp.bfloat16), 'lat').astype(jnp.float32)  84.3 us
    all_gather x1, waiting for transfers between devices, local(): heads_full = lax.all_gather(head_weight, 'lat', axis=1, tiled=True)  48.6 us
    unnamed x5, waiting for transfers between devices  34.2 us
    all_gather x1, waiting for transfers between devices, local(): piece = lax.all_gather(latent, 'var', axis=1, tiled=True)  28.4 us
    unnamed x32, local copies, waits for them, and re-layouts  16.3 us
    dot_general x1, matrix products, slot_terms(): jnp.einsum('krnd,kdo->krno', rows, heads_full, preferred_element_type=jnp...  10.1 us
    dot_general x1, matrix products, slot_terms(): jnp.einsum('krno,kdo->krnd', errors, heads_full, preferred_element_type=j...  9.86 us
    another operation x2, local copies, waits for them, and re-layouts, split(): shaped = values.reshape(win_rows, WH, win_cols, WW, parts, heads, head_size)  8.98 us
  transfers between devices with their start and end apart: 8, of which 7 were waited for; matrix products, arithmetic and copies ran while one was open for 6% of the time, Pallas kernels for 0%

commit v1 on v0

--- a/solution.py
+++ b/solution.py
@@ -132,7 +132,9 @@
     live_tiles = (slot_level[None, :] < tile_levels[:, None]).astype(jnp.float32)
     heads_full = lax.all_gather(head_weight, "lat", axis=1, tiled=True)
     tile_ids = jnp.arange(var_count, dtype=jnp.int32)
-    piece = lax.all_gather(latent, "var", axis=1, tiled=True)
+    piece = jnp.concatenate(
+        lax.all_to_all(jnp.stack([latent] * lax.axis_size("var")), "var", 0, 0), axis=1
+    )
     piece_cols = piece.shape[1]
     column_tile = jnp.arange(piece_cols, dtype=jnp.int32) // band_cols
     onehot = (column_tile[:, None] == tile_ids[None, :]).astype(jnp.float32)

time: 329 us -> 289 us (0.88)
  waiting for transfers between devices: 204 us -> 156 us
  starting transfers between devices: 7.98 us -> 13.9 us
    all_gather x1, waiting for transfers between devices: 48.6 us -> 0.01 us  [local(): heads_full = lax.all_gather(head_weight, 'lat', axis=1, tiled=True)]
    all_to_all x0 -> x1, waiting for transfers between devices: none -> 29.5 us  [local(): lax.all_to_all(jnp.stack([latent] * lax.axis_size('var')), 'var', 0, 0)]
    all_gather x1 -> x0, waiting for transfers between devices: 28.4 us -> none  [local(): piece = lax.all_gather(latent, 'var', axis=1, tiled=True)]
    all_to_all x0 -> x1, starting transfers between devices: none -> 5.73 us  [local(): lax.all_to_all(jnp.stack([latent] * lax.axis_size('var')), 'var', 0, 0)]
    unnamed x5 -> x4, waiting for transfers between devices: 34.2 us -> 33.6 us
    unnamed x32 -> x34, local copies, waits for them, and re-layouts: 16.3 us -> 16.3 us
  transfers between devices with their start and end apart: 8 -> 8, of which waited for: 7 -> 6; matrix products, arithmetic and copies ran while one was open for 6% -> 28% of each run, Pallas kernels for 0% -> 0%
where the time goes in v1:
time: 289 us; the launch traced here: 288 us
  waiting for transfers between devices  156 us (54%)
  local copies, waits for them, and re-layouts  49.9 us (17%)
  matrix products  41 us (14%)
  between operations  14 us (5%)
  starting transfers between devices  13.9 us (5%)
  other arithmetic  12.7 us (4%)
    psum x1, waiting for transfers between devices, local(): lax.psum(head_terms.astype(jnp.bfloat16), 'lat').astype(jnp.float32)  85 us
    unnamed x4, waiting for transfers between devices  33.6 us
    all_to_all x1, waiting for transfers between devices, local(): lax.all_to_all(jnp.stack([latent] * lax.axis_size('var')), 'var', 0, 0)  29.5 us
    unnamed x34, local copies, waits for them, and re-layouts  16.3 us
    dot_general x1, matrix products, slot_terms(): jnp.einsum('krnd,kdo->krno', rows, heads_full, preferred_element_type=jnp...  9.92 us
    dot_general x1, matrix products, slot_terms(): jnp.einsum('krno,kdo->krnd', errors, heads_full, preferred_element_type=j...  9.86 us
    another operation x2, local copies, waits for them, and re-layouts, split(): shaped = values.reshape(win_rows, WH, win_cols, WW, parts, heads, head_size)  9.06 us
    dot_general x1, matrix products, slot_terms(): jnp.einsum('krnd,krno->dko', rows, errors, preferred_element_type=jnp.flo...  6.63 us
  transfers between devices with their start and end apart: 8, of which 6 were waited for; matrix products, arithmetic and copies ran while one was open for 28% of the time, Pallas kernels for 0%

profile of v1, /device:TPU:0, one launch (start us, length us, event | category | flops | bytes accessed | tf_op | source)
XLA Modules:
  0.0 287.7 jit_solution(17823371605606555132)
XLA Ops:
  8.4 3.6 %collective-permute-start = (bf16[3,24,1024]{2,1,0:T(8,128)(2,1)S(1)}, bf16[3,24,1024]{2,1,0:T(8,128)(2,1)S(1)}, u32[]{:S(2)}, u32[]{:S(2)}) collective-permute-start(bf16[3,24,1024]{2,1,0:T(8,128)(2,1)S(1)} %get-tuple-element.28), channel_id=1, source_target_pairs={{0,8},{8,16},{16,24},{24,32},{32,40},{40,48},{48,56},{56,64},{64,7... | collective-permute-start | bytes 442376 | tf_op jit(solution)/shard_map/ppermute | solution.py:20
  16.0 3.1 %collective-permute-done.1 = bf16[3,24,1024]{2,1,0:T(8,128)(2,1)S(1)} collective-permute-done((bf16[3,24,1024]{2,1,0:T(8,128)(2,1)S(1)}, bf16[3,24,1024]{2,1,0:T(8,128)(2,1)S(1)}, u32[]{:S(2)}, u32[]{:S(2)}) %collective-permute-start.1) | collective-permute-done | bytes 147488 | tf_op jit(solution)/shard_map/ppermute | solution.py:21
  19.3 2.9 %collective-permute-start.3 = (bf16[12,6,1024]{2,1,0:T(8,128)(2,1)S(1)}, bf16[12,6,1024]{2,1,0:T(8,128)(2,1)S(1)}, u32[]{:S(2)}, u32[]{:S(2)}) collective-permute-start(bf16[12,6,1024]{2,1,0:T(8,128)(2,1)S(1)} %get-tuple-element.26), channel_id=1, source_target_pairs={{1,0},{2,1},{3,2},{4,3},{5,4},{6,5},{7,6},{0,7},{9,8},{10,9},{11,1... | collective-permute-start | bytes 442376 | tf_op jit(solution)/shard_map/ppermute | solution.py:21
  22.4 3.1 %collective-permute-done.2 = bf16[12,6,1024]{2,1,0:T(8,128)(2,1)S(1)} collective-permute-done((bf16[12,6,1024]{2,1,0:T(8,128)(2,1)S(1)}, bf16[12,6,1024]{2,1,0:T(8,128)(2,1)S(1)}, u32[]{:S(2)}, u32[]{:S(2)}) %collective-permute-start.2) | collective-permute-done | bytes 147488 | tf_op jit(solution)/shard_map/ppermute | solution.py:20
  29.8 2.7 reshape.112
  33.7 2.2 fusion.40
  38.2 3.2 %copy.57 = bf16[2,3,6,12,1,16,64]{6,5,3,2,1,0,4:T(8,128)(2,1)} copy(bf16[2,3,6,12,1,16,64]{6,5,3,1,2,0,4:T(8,128)(2,1)} %bitcast.61) | data formatting | bytes 1769472 | tf_op jit(solution)/shard_map/transpose | solution.py:42
  41.5 5.5 %fusion.15 = bf16[432,2048]{1,0:T(8,128)(2,1)} fusion(bf16[1024,3072]{1,0:T(8,128)(2,1)} %param.13, f32[432,1024]{1,0:T(8,128)S(1)} %copy-done.3, f32[1024]{0:T(1024)S(1)} %copy-done.6, f32[432]{0:T(512)S(1)} %rsqrt.13, f32[432]{0:T(512)S(1)} %div.33), kind=kOutput, calls=%fused_computation.22 | convolution fusion | flops 1814593536 | bytes 7740800 | tf_op jit(solution)/shard_map/dot_general | solution.py:107
  47.0 6.5 %reshape_reshape.3 = bf16[2,6,3,12,2,16,64]{6,5,4,3,2,1,0:T(8,128)(2,1)} reshape(bf16[432,2048]{1,0:T(8,128)(2,1)} %fusion.15) | data formatting | bytes 3538944 | tf_op jit(solution)/shard_map/reshape;reshape | solution.py:41
  53.4 2.6 copy.55
  56.0 2.7 fusion.59
  58.7 4.0 %copy.70 = bf16[6,72,1,16,64]{1,4,3,0,2:T(8,128)(2,1)} copy(bf16[6,72,1,16,64]{4,3,2,1,0:T(8,128)(2,1)} %get-tuple-element.21) | data formatting | bytes 1769472
  62.8 4.1 %copy.71 = bf16[6,72,1,16,64]{1,4,3,0,2:T(8,128)(2,1)} copy(bf16[6,72,1,16,64]{4,3,2,1,0:T(8,128)(2,1)} %get-tuple-element.22) | data formatting | bytes 1769472
  66.8 3.1 %fusion.25 = f32[6,16,72,72]{2,3,1,0:T(8,128)S(1)} fusion(bf16[6,72,16,64]{3,2,1,0:T(8,128)(2,1)} %bitcast.62, bf16[6,72,1,16,64]{1,4,3,0,2:T(8,128)(2,1)} %copy.71), kind=kOutput, calls=%fused_computation.30 | convolution fusion | flops 63700992 | bytes 3760128 | tf_op jit(solution)/shard_map/wqhd,wkhd->whqk/dot_general | solution.py:53
  73.7 4.0 %copy.61 = bf16[6,72,16,64]{3,2,1,0:T(8,128)(2,1)} copy(bf16[6,72,16,64]{1,3,2,0:T(8,128)(2,1)} %fusion.34) | data formatting | bytes 1769472 | tf_op jit(solution)/shard_map/whqk,wkhd->wqhd/transpose | solution.py:60
  77.7 3.9 %reshape.110 = bf16[2,3,6,12,1024]{4,3,2,1,0:T(8,128)(2,1)} reshape(bf16[6,72,16,64]{3,2,1,0:T(8,128)(2,1)} %copy.61) | data formatting | bytes 1769472 | tf_op jit(solution)/shard_map/reshape | solution.py:62
  87.4 5.7 %all-to-all-start = ((bf16[8,6,24,1024]{3,2,1,0:T(8,128)(2,1)}), bf16[8,6,24,1024]{3,2,1,0:T(8,128)(2,1)}, u32[]{:S(2)}, u32[]{:S(2)}) async-start(bf16[8,6,24,1024]{3,2,1,0:T(8,128)(2,1)} %stack.2), calls=%async_computation | async-start | bytes 4718592 | tf_op jit(solution)/shard_map/all_to_all | solution.py:136
  93.8 29.5 %all-to-all-done = bf16[8,6,24,1024]{3,2,1,0:T(8,128)(2,1)} async-done(((bf16[8,6,24,1024]{3,2,1,0:T(8,128)(2,1)}), bf16[8,6,24,1024]{3,2,1,0:T(8,128)(2,1)}, u32[]{:S(2)}, u32[]{:S(2)}) %all-to-all-start) | async-done | bytes 2359328 | tf_op jit(solution)/shard_map/all_to_all | solution.py:136
  123.3 4.4 %copy_convert_fusion = f32[8,6,24,1024]{3,2,0,1:T(8,128)} fusion(bf16[8,6,24,1024]{3,2,1,0:T(8,128)(2,1)} %all-to-all-done), kind=kLoop, calls=%fused_computation.24 | loop fusion | flops 1179648 | bytes 7077888 | tf_op jit(solution)/shard_map/convert_element_type | solution.py:69
  127.7 9.9 %multiply_convert_fusion = bf16[5,6,192,320]{3,2,1,0:T(8,128)(2,1)S(1)} fusion(bf16[5,6,192,320]{3,2,1,0:T(8,128)(2,1)} %param.18, f32[5,192]{1,0:T(8,128)S(1)} %fusion.52, bf16[5,1024,320]{2,1,0:T(8,128)(2,1)} %all-gather.2.cloned.1.call-done, f32[5,1024]{1,0:T(8,128)S(1)} %copy-done.7, f32[5,1024]{1,0:T(8,128)S(1)} %copy-done.8, f32[6,192,1024]{2,1,0:T(8,128)} %bitcast.63), kind=kOutput, calls=%fused_computation.11 | convolution fusion | flops 3799941120 | bytes 15412992 | tf_op jit(solution)/shard_map/krnd,kdo->krno/dot_general | solution.py:73
  139.7 6.6 %fusion.14 = bf16[1024,5,320]{0,2,1:T(8,128)(2,1)} fusion(bf16[5,6,192,320]{3,2,1,0:T(8,128)(2,1)S(1)} %multiply_convert_fusion, f32[5,1024]{1,0:T(8,128)S(1)} %copy-done.7, f32[5,1024]{1,0:T(8,128)S(1)} %copy-done.8, f32[6,192,1024]{2,1,0:T(8,128)S(1)} %bitcast.64), kind=kOutput, calls=%fused_computation.21 | convolution fusion | flops 3795845120 | bytes 11722752 | tf_op jit(solution)/shard_map/krnd,krno->dko/dot_general | solution.py:79
  146.4 9.9 %multiply_reduce_fusion = bf16[6,192,1024]{2,1,0:T(8,128)(2,1)S(1)} fusion(f32[5,1024]{1,0:T(8,128)S(1)} %copy-done.8, bf16[5,6,192,320]{3,2,1,0:T(8,128)(2,1)} %copy-done.12, bf16[5,1024,320]{2,1,0:T(8,128)(2,1)} %all-gather.2.cloned.1.call-done), kind=kOutput, calls=%fused_computation.1 | convolution fusion | flops 3785490432 | bytes 9342976 | tf_op jit(solution)/shard_map/krno,kdo->krnd/dot_general | solution.py:77
  158.0 85.0 %all-reduce.3.cloned.1.call-done = bf16[1024,5,320]{0,2,1:T(8,128)(2,1)} async-done(((bf16[1024,5,320]{0,2,1:T(8,128)(2,1)}), bf16[1024,5,320]{0,2,1:T(8,128)(2,1)}) %all-reduce.3.cloned.1.call-update) | async-done | bytes 3276816 | tf_op jit(solution)/shard_map/psum | solution.py:152
  245.3 33.6 %reduce-scatter.4.cloned.1.call-done = bf16[24,6144]{1,0:T(8,128)(2,1)} async-done(((bf16[192,6144]{1,0:T(8,128)(2,1)}), bf16[24,6144]{1,0:T(8,128)(2,1)}) %reduce-scatter.4.cloned.1.call-update) | async-done | bytes 294928
  (70 shorter events, 31.7 us)
Async XLA Ops:
  7.2 76.9 %copy-start = (bf16[1024,1024]{1,0:T(8,128)(2,1)S(1)}, bf16[1024,1024]{1,0:T(8,128)(2,1)}, u32[]{:S(2)}) copy-start(bf16[1024,1024]{1,0:T(8,128)(2,1)} %param.14) | copy-start | bytes 6291460
  7.2 120.5 %all-gather.2.cloned.1.call-start = ((), (), s32[]{:S(2)}) async-start(), calls=%async_computation.2 | async-start | bytes 4177920 | tf_op jit(solution)/shard_map/all_gather | solution.py:133
  8.4 6.7 %collective-permute-start = (bf16[3,24,1024]{2,1,0:T(8,128)(2,1)S(1)}, bf16[3,24,1024]{2,1,0:T(8,128)(2,1)S(1)}, u32[]{:S(2)}, u32[]{:S(2)}) collective-permute-start(bf16[3,24,1024]{2,1,0:T(8,128)(2,1)S(1)} %get-tuple-element.28), channel_id=1, source_target_pairs={{0,8},{8,16},{16,24},{24,32},{32,40},{40,48},{48,56},{56,64},{64,7... | collective-permute-start | bytes 442376 | tf_op jit(solution)/shard_map/ppermute | solution.py:20
  12.0 7.2 %collective-permute-start.1 = (bf16[3,24,1024]{2,1,0:T(8,128)(2,1)S(1)}, bf16[3,24,1024]{2,1,0:T(8,128)(2,1)S(1)}, u32[]{:S(2)}, u32[]{:S(2)}) collective-permute-start(bf16[3,24,1024]{2,1,0:T(8,128)(2,1)S(1)} %get-tuple-element.27), channel_id=1, source_target_pairs={{8,0},{16,8},{24,16},{32,24},{40,32},{48,40},{56,48},{64,56},{72,6... | collective-permute-start | bytes 442376 | tf_op jit(solution)/shard_map/ppermute | solution.py:21
  19.2 6.3 %collective-permute-start.2 = (bf16[12,6,1024]{2,1,0:T(8,128)(2,1)S(1)}, bf16[12,6,1024]{2,1,0:T(8,128)(2,1)S(1)}, u32[]{:S(2)}, u32[]{:S(2)}) collective-permute-start(bf16[12,6,1024]{2,1,0:T(8,128)(2,1)S(1)} %get-tuple-element.25), channel_id=1, source_target_pairs={{0,1},{1,2},{2,3},{3,4},{4,5},{5,6},{6,7},{7,0},{8,9},{9,10},{10,1... | collective-permute-start | bytes 442376 | tf_op jit(solution)/shard_map/ppermute | solution.py:20
  19.3 6.3 %collective-permute-start.3 = (bf16[12,6,1024]{2,1,0:T(8,128)(2,1)S(1)}, bf16[12,6,1024]{2,1,0:T(8,128)(2,1)S(1)}, u32[]{:S(2)}, u32[]{:S(2)}) collective-permute-start(bf16[12,6,1024]{2,1,0:T(8,128)(2,1)S(1)} %get-tuple-element.26), channel_id=1, source_target_pairs={{1,0},{2,1},{3,2},{4,3},{5,4},{6,5},{7,6},{0,7},{9,8},{10,9},{11,1... | collective-permute-start | bytes 442376 | tf_op jit(solution)/shard_map/ppermute | solution.py:21
  27.9 4.5 %copy-start.6 = (f32[1024]{0:T(1024)S(1)}, f32[1024]{0:T(1024)}, u32[]{:S(2)}) copy-start(f32[1024]{0:T(1024)} %param.12) | copy-start | bytes 12292
  38.2 3.2 %copy-start.3 = (f32[432,1024]{1,0:T(8,128)S(1)}, f32[432,1024]{1,0:T(8,128)}, u32[]{:S(2)}) copy-start(f32[432,1024]{1,0:T(8,128)} %reshape.112) | copy-start | bytes 5308420
  70.0 1.8 copy-start.4
  85.7 1.7 copy-start.5
  85.7 7.7 %copy-start.9 = (s32[4]{0:T(128)S(1)}, s32[4]{0:T(128)}, u32[]{:S(2)}) copy-start(s32[4]{0:T(128)} %param.19) | copy-start | bytes 52
  85.7 7.7 %copy-start.10 = (s32[1,8]{1,0:T(1,128)S(1)}, s32[1,8]{1,0:T(1,128)}, u32[]{:S(2)}) copy-start(s32[1,8]{1,0:T(1,128)} %param.20) | copy-start | bytes 100
  85.7 7.8 %copy-start.11 = (s32[5]{0:T(128)S(1)}, s32[5]{0:T(128)}, u32[]{:S(2)}) copy-start(s32[5]{0:T(128)} %param.21) | copy-start | bytes 64
  87.4 35.8 %all-to-all-start = ((bf16[8,6,24,1024]{3,2,1,0:T(8,128)(2,1)}), bf16[8,6,24,1024]{3,2,1,0:T(8,128)(2,1)}, u32[]{:S(2)}, u32[]{:S(2)}) async-start(bf16[8,6,24,1024]{3,2,1,0:T(8,128)(2,1)} %stack.2), calls=%async_computation | async-start | bytes 4718592 | tf_op jit(solution)/shard_map/all_to_all | solution.py:136
  93.2 149.9 %all-reduce.3.cloned.1.call-start = ((), (), s32[]{:S(2)}) async-start(), calls=%async_computation.3 | async-start | bytes 6553600 | tf_op jit(solution)/shard_map/psum | solution.py:152
  93.8 33.9 %copy-start.7 = (f32[5,1024]{1,0:T(8,128)S(1)}, f32[5,1024]{1,0:T(8,128)}, u32[]{:S(2)}) copy-start(f32[5,1024]{1,0:T(8,128)} %param.16) | copy-start | bytes 61444
  93.8 33.9 %copy-start.8 = (f32[5,1024]{1,0:T(8,128)S(1)}, f32[5,1024]{1,0:T(8,128)}, u32[]{:S(2)}) copy-start(f32[5,1024]{1,0:T(8,128)} %param.15) | copy-start | bytes 61444
  127.7 12.1 %copy-start.2 = (f32[8,6,24,1024]{3,2,0,1:T(8,128)S(1)}, f32[8,6,24,1024]{3,2,0,1:T(8,128)}, u32[]{:S(2)}) copy-start(f32[8,6,24,1024]{3,2,0,1:T(8,128)} %copy_convert_fusion) | copy-start | bytes 14155780
  137.6 2.2 copy-start.12
  146.4 132.5 %reduce-scatter.4.cloned.1.call-start = ((), (), s32[]{:S(2)}) async-start(), calls=%async_computation.4 | async-start | bytes 2654208
  156.3 124.8 %copy-start.1 = (bf16[1024,1024]{1,0:T(8,128)(2,1)S(1)}, bf16[1024,1024]{1,0:T(8,128)(2,1)}, u32[]{:S(2)}) copy-start(bf16[1024,1024]{1,0:T(8,128)(2,1)} %param.14) | copy-start | bytes 6291460
Sparse Core Ops, SparseCore 0:
  22.3 52.7 all-gather.1
  146.5 96.4 all-reduce.2
  245.6 33.2 reduce-scatter.3
